TPU v7x, 32 devices: a whole 2x2x4 slice. The times are simulated.
32 devices in a mesh: row: 4 (over x, core), col: 8 (over z, y).
Axes of the slice: x: 2, y: 2, z: 4, core: 2. Of those that a mesh axis runs over, the one named last changes fastest.
Arguments:
- inputs: bfloat16 [512, 6144], P('col', 'row'), may hold values from -6 to 6
- cotangent: bfloat16 [512, 6144], P('col', 'row'), may hold values from -6 to 6
- weight_in: bfloat16 [6144, 12288], P('row', 'col'), may hold values from -0.078125 to 0.078125
- moment_in: bfloat16 [6144, 12288], P('row', 'col'), may hold values from -5 to 5
- second_in: bfloat16 [6144, 12288], P('row', 'col'), may hold values from 0.049804688 to 2
- weight_out: bfloat16 [12288, 6144], P('col', 'row'), may hold values from -0.0546875 to 0.0546875
- moment_out: bfloat16 [12288, 6144], P('col', 'row'), may hold values from -5 to 5
- second_out: bfloat16 [12288, 6144], P('col', 'row'), may hold values from 0.049804688 to 2
Outputs:
- input_grad: bfloat16 [512, 6144], P('col', 'row')
- update_in: bfloat16 [6144, 12288], P('row', 'col')
- code_moment_in: bfloat16 [6144, 12288], P('row', 'col')
- code_second_in: bfloat16 [6144, 12288], P('row', 'col')
- row_scale_in: float32 [2, 6144], P(None, 'row')
- col_scale_in: float32 [2, 12288], P(None, 'col')
- update_out: bfloat16 [12288, 6144], P('col', 'row')
- code_moment_out: bfloat16 [12288, 6144], P('col', 'row')
- code_second_out: bfloat16 [12288, 6144], P('col', 'row')
- row_scale_out: float32 [2, 12288], P(None, 'col')
- col_scale_out: float32 [2, 6144], P(None, 'row')
All inputs are finite; a program needn't handle non-finite values. Where the computation divides by a largest or mean magnitude, that divisor is 1e-20 or more.
Results may differ from a plain program's by a relative error of at most 0.0049.
Values may be sent and summed in bfloat16 or wider, within the bound.
A program may use at most 192 MiB of HBM per device.

v0:
```python
import jax
import jax.numpy as jnp
from jax import lax
from jax.sharding import PartitionSpec as P

D = 6144
FF = 12288


root_half = 0.7071067811865476
normal_density = 0.3989422804014327
momentum_decay = 0.9
second_decay = 0.95
stable_eps = 1e-08
weight_decay = 0.1


def contract(left, right, left_dim, right_dim):
    return lax.dot_general(
        left, right, (((left_dim,), (right_dim,)), ((), ())), preferred_element_type=jnp.float32
    )


def activate(preact, hidden_grad):
    cumulative = 0.5 * (1.0 + lax.erf(preact * root_half))
    density = jnp.exp(-0.5 * preact * preact) * normal_density
    hidden = (preact * cumulative).astype(jnp.bfloat16)
    delta = (hidden_grad * (cumulative + preact * density)).astype(jnp.bfloat16)
    return (hidden, delta)


def moments(weight, moment, second, gradient, factor):
    scaled = gradient * factor
    moment_new = momentum_decay * moment.astype(jnp.float32) + (1.0 - momentum_decay) * scaled
    second_new = second_decay * second.astype(jnp.float32) + (1.0 - second_decay) * scaled * scaled
    update = moment_new / (jnp.sqrt(second_new) + stable_eps) + weight_decay * weight.astype(
        jnp.float32
    )
    row_local = jnp.stack([jnp.max(jnp.abs(moment_new), axis=1), jnp.max(second_new, axis=1)])
    col_local = jnp.stack([jnp.max(jnp.abs(moment_new), axis=0), jnp.max(second_new, axis=0)])
    return (update.astype(jnp.bfloat16), moment_new, second_new, row_local, col_local)


def encode(moment_new, second_new, row_top, col_top):
    row_top = jnp.maximum(row_top, 1.0)
    col_top = jnp.maximum(col_top, 1.0)
    code_moment = moment_new / jnp.minimum(row_top[0][:, None], col_top[0][None, :])
    code_second = second_new / jnp.minimum(row_top[1][:, None], col_top[1][None, :])
    return (code_moment.astype(jnp.bfloat16), code_second.astype(jnp.bfloat16), row_top, col_top)


def shards(inputs, cotangent, weight_in, moment_in, second_in, weight_out, moment_out, second_out):
    all_inputs, all_cotangent = (
        lax.all_gather(inputs, "col", axis=0, tiled=True),
        lax.all_gather(cotangent, "col", axis=0, tiled=True),
    )
    hidden_cols = weight_in.shape[1]
    preact_part = jnp.dot(all_inputs, weight_in, preferred_element_type=jnp.float32)
    grad_part = contract(all_cotangent, weight_out, 1, 1)
    stacked = lax.psum_scatter(
        jnp.concatenate([preact_part, grad_part], axis=1), "row", scatter_dimension=0, tiled=True
    )
    hidden, delta = activate(stacked[:, :hidden_cols], stacked[:, hidden_cols:])
    all_hidden, all_delta = (
        lax.all_gather(hidden, "row", axis=0, tiled=True),
        lax.all_gather(delta, "row", axis=0, tiled=True),
    )
    input_grad = lax.psum_scatter(
        contract(all_delta, weight_in, 1, 1), "col", scatter_dimension=0, tiled=True
    )
    input_grad = input_grad.astype(jnp.bfloat16)
    grad_in = contract(all_inputs, all_delta, 0, 0)
    grad_out = contract(all_hidden, all_cotangent, 0, 0)
    local_total = jnp.sum(grad_in * grad_in) + jnp.sum(grad_out * grad_out)
    total = lax.psum(local_total, ("row", "col"))
    factor = 1.0 / jnp.maximum(jnp.sqrt(total / (2.0 * D * FF)), 1.0)
    update_in, moment_new_in, second_new_in, rows_in, cols_in = moments(
        weight_in, moment_in, second_in, grad_in, factor
    )
    update_out, moment_new_out, second_new_out, rows_out, cols_out = moments(
        weight_out, moment_out, second_out, grad_out, factor
    )
    rows_in, cols_out = lax.pmax((rows_in, cols_out), "col")
    cols_in, rows_out = lax.pmax((cols_in, rows_out), "row")
    code_moment_in, code_second_in, row_scale_in, col_scale_in = encode(
        moment_new_in, second_new_in, rows_in, cols_in
    )
    code_moment_out, code_second_out, row_scale_out, col_scale_out = encode(
        moment_new_out, second_new_out, rows_out, cols_out
    )
    return (
        input_grad,
        update_in,
        code_moment_in,
        code_second_in,
        row_scale_in,
        col_scale_in,
        update_out,
        code_moment_out,
        code_second_out,
        row_scale_out,
        col_scale_out,
    )


def solution(mesh):
    in_specs = (
        P("col", "row"),
        P("col", "row"),
        P("row", "col"),
        P("row", "col"),
        P("row", "col"),
        P("col", "row"),
        P("col", "row"),
        P("col", "row"),
    )
    out_specs = (
        P("col", "row"),
        P("row", "col"),
        P("row", "col"),
        P("row", "col"),
        P(None, "row"),
        P(None, "col"),
        P("col", "row"),
        P("col", "row"),
        P("col", "row"),
        P(None, "col"),
        P(None, "row"),
    )
    return jax.shard_map(shards, mesh=mesh, in_specs=in_specs, out_specs=out_specs, check_vma=False)
```

profile of v0, /device:TPU:0, one launch (start us, length us, event | category | flops | bytes accessed | tf_op | source)
XLA Modules:
  0.0 432.1 jit_solution(10932601547169694082)
XLA Ops:
  8.7 48.4 %all-gather.7.cloned.1.call-done = bf16[512,1536]{1,0:T(8,128)(2,1)} async-done(((bf16[64,1536]{1,0:T(8,128)(2,1)}), bf16[512,1536]{1,0:T(8,128)(2,1)}) %all-gather.7.cloned.1.call-update) | async-done | bytes 1572880 | tf_op jit(solution)/shard_map/all_gather | solution.py:55
  62.1 39.8 %all-gather.5.cloned.1.call-done = bf16[512,1536]{1,0:T(8,128)(2,1)} async-done(((bf16[64,1536]{1,0:T(8,128)(2,1)}), bf16[512,1536]{1,0:T(8,128)(2,1)}) %all-gather.5.cloned.1.call-update) | async-done | bytes 1572880 | tf_op jit(solution)/shard_map/all_gather | solution.py:54
  110.1 57.3 %reduce-scatter.3.cloned.1.call-done = f32[128,3072]{1,0:T(8,128)} async-done(((f32[512,3072]{1,0:T(8,128)}), f32[128,3072]{1,0:T(8,128)}) %reduce-scatter.3.cloned.1.call-update) | async-done | bytes 1572880 | tf_op jit(solution)/shard_map/reduce_scatter | solution.py:60
  170.7 6.6 %copy.22 = bf16[1536,1536]{0,1:T(8,128)(2,1)} copy(bf16[1536,1536]{1,0:T(8,128)(2,1)} %param.10) | data formatting | bytes 9437184 | tf_op args[2]
  177.3 6.9 %copy.26 = bf16[1536,1536]{0,1:T(8,128)(2,1)} copy(bf16[1536,1536]{1,0:T(8,128)(2,1)} %param.13) | data formatting | bytes 9437184 | tf_op args[5]
  184.2 6.6 %copy.19 = bf16[1536,1536]{0,1:T(8,128)(2,1)} copy(bf16[1536,1536]{1,0:T(8,128)(2,1)} %param.11) | data formatting | bytes 9437184 | tf_op args[3]
  190.8 6.6 %copy.21 = bf16[1536,1536]{0,1:T(8,128)(2,1)} copy(bf16[1536,1536]{1,0:T(8,128)(2,1)} %param.12) | data formatting | bytes 9437184 | tf_op args[4]
  197.4 6.8 %copy.23 = bf16[1536,1536]{0,1:T(8,128)(2,1)} copy(bf16[1536,1536]{1,0:T(8,128)(2,1)} %param.14) | data formatting | bytes 9437184 | tf_op args[6]
  204.2 6.6 %copy.25 = bf16[1536,1536]{0,1:T(8,128)(2,1)} copy(bf16[1536,1536]{1,0:T(8,128)(2,1)} %param.15) | data formatting | bytes 9437184 | tf_op args[7]
  210.9 7.7 %multiply_reduce_fusion.1 = (f32[]{:T(128)}, f32[1536,1536]{1,0:T(8,128)}) fusion(bf16[512,1536]{1,0:T(8,128)(2,1)} %all-gather.9.cloned.1.call-done, bf16[512,1536]{1,0:T(8,128)(2,1)S(1)} %copy-done.5), kind=kOutput, calls=%fused_computation.14 | convolution fusion | flops 2420637696 | bytes 12582916 | tf_op jit(solution)/shard_map/dot_general | solution.py:19
  218.6 7.6 %multiply_reduce_fusion = (f32[]{:T(128)}, f32[1536,1536]{1,0:T(8,128)}) fusion(bf16[512,1536]{1,0:T(8,128)(2,1)} %all-gather.11.cloned.1.call-done, bf16[512,1536]{1,0:T(8,128)(2,1)S(1)} %copy-done.4), kind=kOutput, calls=%fused_computation.13 | convolution fusion | flops 2420637696 | bytes 12582916 | tf_op jit(solution)/shard_map/dot_general | solution.py:19
  234.1 41.7 %psum.7 = f32[]{:T(128)} all-reduce(f32[]{:T(128)S(6)} %add.45), channel_id=1, replica_groups=mesh['row'=4,'col'=8] {'row','col'}, use_global_device_ids=true, to_apply=%region_4.0 | all-reduce | flops 1 | bytes 8 | tf_op jit(solution)/shard_map/psum | solution.py:75
  276.5 14.6 %abs_reduce_fusion.3 = (f32[1536]{0:T(1024)S(1)}, f32[1536]{0:T(1024)S(1)}, f32[1536]{0:T(1024)S(1)}, f32[1536]{0:T(1024)S(1)}, bf16[1536,1536]{0,1:T(8,128)(2,1)}) fusion(f32[1536,1536]{1,0:T(8,128)} %get-tuple-element.55, f32[]{:T(128)S(6)} %div.25, bf16[1536,1536]{0,1:T(8,128)(2,1)} %copy.19, bf16[1536,1536]{0,1:T(8,128)(2,1)} %copy.21, ...), kind=kLoop, calls=%fused_computation.18 | loop fusion | flops 49539072 | bytes 28336132 | tf_op jit(solution)/shard_map/reduce_max | solution.py:39
  291.1 6.6 %copy.27 = bf16[1536,1536]{1,0:T(8,128)(2,1)} copy(bf16[1536,1536]{0,1:T(8,128)(2,1)} %get-tuple-element.47) | data formatting | bytes 9437184
  297.7 9.7 %copy.24 = f32[1536,1536]{0,1:T(8,128)} copy(f32[1536,1536]{1,0:T(8,128)} %get-tuple-element.57) | data formatting | bytes 18874368 | tf_op jit(solution)/shard_map/dot_general | solution.py:19
  307.4 14.5 %abs_reduce_fusion.1 = (f32[1536]{0:T(1024)S(1)}, f32[1536]{0:T(1024)S(1)}, f32[1536]{0:T(1024)S(1)}, f32[1536]{0:T(1024)S(1)}, bf16[1536,1536]{0,1:T(8,128)(2,1)}) fusion(f32[1536,1536]{0,1:T(8,128)} %copy.24, f32[]{:T(128)S(6)} %div.25, bf16[1536,1536]{0,1:T(8,128)(2,1)} %copy.23, bf16[1536,1536]{0,1:T(8,128)(2,1)} %copy.25, bf16[1536,1536]{0,1:T(8,128)(2,1)} %copy.26), kind=kLoop, calls=%fused_computation.16 | loop fusion | flops 49539072 | bytes 28336132 | tf_op jit(solution)/shard_map/reduce_max | solution.py:39
  322.0 36.4 %all-reduce = (f32[2,1536]{1,0:T(2,128)S(1)}, f32[2,1536]{1,0:T(2,128)S(1)}) all-reduce(f32[2,1536]{1,0:T(2,128)S(1)} %pad_maximum_fusion.1, f32[2,1536]{1,0:T(2,128)S(1)} %pad_maximum_fusion.4), channel_id=1, replica_groups=mesh['row'=4,'col'=8] {'col'}, use_global_device_ids=true, to_apply=%region_7.0 | all-reduce | flops 6144 | bytes 49152 | tf_op jit(solution)/shard_map/pmax | solution.py:83
  358.6 10.5 %all-reduce.1 = (f32[2,1536]{1,0:T(2,128)S(1)}, f32[2,1536]{1,0:T(2,128)S(1)}) all-reduce(f32[2,1536]{1,0:T(2,128)S(1)} %pad_maximum_fusion.2, f32[2,1536]{1,0:T(2,128)S(1)} %pad_maximum_fusion.3), channel_id=1, replica_groups=mesh['row'=4,'col'=8] {'row'}, use_global_device_ids=true, to_apply=%region_10.0 | all-reduce | flops 6144 | bytes 49152 | tf_op jit(solution)/shard_map/pmax | solution.py:84
  369.3 21.2 %divide_convert_fusion = (bf16[1536,1536]{0,1:T(8,128)(2,1)}, bf16[1536,1536]{0,1:T(8,128)(2,1)}, bf16[1536,1536]{0,1:T(8,128)(2,1)}, bf16[1536,1536]{0,1:T(8,128)(2,1)}) fusion(f32[1536]{0:T(1024)S(1)} %get-tuple-element.36, f32[1536]{0:T(1024)S(1)} %get-tuple-element.34, f32[1536,1536]{0,1:T(8,128)} %copy.24, f32[]{:T(128)S(6)} %div.25, ...), kind=kLoop, calls=%fused_computation.6 | loop fusion | flops 75497472 | bytes 56672260 | tf_op jit(solution)/shard_map/convert_element_type | solution.py:49
  390.5 6.6 %copy.28 = bf16[1536,1536]{1,0:T(8,128)(2,1)} copy(bf16[1536,1536]{0,1:T(8,128)(2,1)} %get-tuple-element.58) | data formatting | bytes 9437184
  397.1 6.6 %copy.29 = bf16[1536,1536]{1,0:T(8,128)(2,1)} copy(bf16[1536,1536]{0,1:T(8,128)(2,1)} %get-tuple-element.59) | data formatting | bytes 9437184
  403.7 6.6 %copy.30 = bf16[1536,1536]{1,0:T(8,128)(2,1)} copy(bf16[1536,1536]{0,1:T(8,128)(2,1)} %get-tuple-element.46) | data formatting | bytes 9437184
  410.3 6.6 %copy.31 = bf16[1536,1536]{1,0:T(8,128)(2,1)} copy(bf16[1536,1536]{0,1:T(8,128)(2,1)} %get-tuple-element.49) | data formatting | bytes 9437184
  416.9 6.6 %copy.32 = bf16[1536,1536]{1,0:T(8,128)(2,1)} copy(bf16[1536,1536]{0,1:T(8,128)(2,1)} %get-tuple-element.48) | data formatting | bytes 9437184
  (55 shorter events, 26.5 us)
Async XLA Ops:
  7.2 49.9 %all-gather.7.cloned.1.call-start = ((), (), s32[]{:S(2)}) async-start(), calls=%async_computation.3 | async-start | bytes 1769472 | tf_op jit(solution)/shard_map/all_gather | solution.py:55
  7.9 94.0 %all-gather.5.cloned.1.call-start = ((), (), s32[]{:S(2)}) async-start(), calls=%async_computation.2 | async-start | bytes 1769472 | tf_op jit(solution)/shard_map/all_gather | solution.py:54
  8.7 158.8 %reduce-scatter.3.cloned.1.call-start = ((), (), s32[]{:S(2)}) async-start(), calls=%async_computation.4 | async-start | bytes 7864320 | tf_op jit(solution)/shard_map/reduce_scatter | solution.py:60
  110.0 100.8 %all-gather.9.cloned.1.call-start = ((), (), s32[]{:S(2)}) async-start(), calls=%async_computation.5 | async-start | bytes 1966080 | tf_op jit(solution)/shard_map/all_gather | solution.py:66
  170.0 48.5 %all-gather.11.cloned.1.call-start = ((), (), s32[]{:S(2)}) async-start(), calls=%async_computation.7 | async-start | bytes 1966080 | tf_op jit(solution)/shard_map/all_gather | solution.py:65
  170.6 252.9 %reduce-scatter.5.cloned.1.call-start = ((), (), s32[]{:S(2)}) async-start(), calls=%async_computation.6 | async-start | bytes 3538944 | tf_op jit(solution)/shard_map/reduce_scatter | solution.py:68
  197.4 13.5 %copy-start.5 = (bf16[512,1536]{1,0:T(8,128)(2,1)S(1)}, bf16[512,1536]{1,0:T(8,128)(2,1)}, u32[]{:S(2)}) copy-start(bf16[512,1536]{1,0:T(8,128)(2,1)} %all-gather.5.cloned.1.call-done) | copy-start | bytes 4718596
  210.9 7.7 %copy-start.4 = (bf16[512,1536]{1,0:T(8,128)(2,1)S(1)}, bf16[512,1536]{1,0:T(8,128)(2,1)}, u32[]{:S(2)}) copy-start(bf16[512,1536]{1,0:T(8,128)(2,1)} %all-gather.7.cloned.1.call-done) | copy-start | bytes 4718596
  218.6 8.9 %copy-start.6 = (bf16[512,1536]{1,0:T(8,128)(2,1)S(1)}, bf16[512,1536]{1,0:T(8,128)(2,1)}, u32[]{:S(2)}) copy-start(bf16[512,1536]{1,0:T(8,128)(2,1)} %all-gather.9.cloned.1.call-done) | copy-start | bytes 4718596
  358.4 32.0 %copy-start = (f32[2,1536]{1,0:T(2,128)}, f32[2,1536]{1,0:T(2,128)S(1)}, u32[]{:S(2)}) copy-start(f32[2,1536]{1,0:T(2,128)S(1)} %broadcast_maximum_fusion) | copy-start | bytes 36868
  369.1 21.4 %copy-start.1 = (f32[2,1536]{1,0:T(2,128)}, f32[2,1536]{1,0:T(2,128)S(1)}, u32[]{:S(2)}) copy-start(f32[2,1536]{1,0:T(2,128)S(1)} %broadcast_maximum_fusion.1) | copy-start | bytes 36868
  369.2 21.3 %copy-start.2 = (f32[2,1536]{1,0:T(2,128)}, f32[2,1536]{1,0:T(2,128)S(1)}, u32[]{:S(2)}) copy-start(f32[2,1536]{1,0:T(2,128)S(1)} %broadcast_maximum_fusion.2) | copy-start | bytes 36868
  369.2 21.2 %copy-start.3 = (f32[2,1536]{1,0:T(2,128)}, f32[2,1536]{1,0:T(2,128)S(1)}, u32[]{:S(2)}) copy-start(f32[2,1536]{1,0:T(2,128)S(1)} %broadcast_maximum_fusion.3) | copy-start | bytes 36868
Sparse Core Ops, SparseCore 0:
  10.2 46.8 all-gather.6
  59.3 42.5 all-gather.4
  110.2 57.2 reduce-scatter.2
  170.2 19.6 all-gather.8
  191.8 19.6 all-gather.10
  234.2 75.4 reduce-scatter.4
where the time goes:
time: 434 us; the launch traced here: 432 us
  waiting for transfers between devices  147 us (34%)
  local copies, waits for them, and re-layouts  89.8 us (21%)
  blocking collectives  88.6 us (20%)
  other arithmetic  57.8 us (13%)
  matrix products  31.8 us (7%)
  between operations  16.4 us (4%)
    unnamed x26, local copies, waits for them, and re-layouts  79.9 us
    reduce_scatter x1, waiting for transfers between devices, shards(): lax.psum_scatter(jnp.concatenate([preact_part, grad_part], axis=1), 'row'...  57.3 us
    all_gather x1, waiting for transfers between devices, shards(): lax.all_gather(cotangent, 'col', axis=0, tiled=True)  48.4 us
    psum x1, blocking collectives, shards(): total = lax.psum(local_total, ('row', 'col'))  41.7 us
    all_gather x1, waiting for transfers between devices, shards(): lax.all_gather(inputs, 'col', axis=0, tiled=True)  39.8 us
    pmax x1, blocking collectives, shards(): rows_in, cols_out = lax.pmax((rows_in, cols_out), 'col')  36.4 us
    reduce_max x2, other arithmetic, moments(): jnp.max(jnp.abs(moment_new), axis=1)  29.1 us
    dot_general x4, matrix products, contract(): lax.dot_general(left, right, (((left_dim,), (right_dim,)), ((), ())), pre...  26.9 us
  transfers between devices with their start and end apart: 6, of which 3 were waited for; matrix products, arithmetic and copies ran while one was open for 35% of the time, Pallas kernels for 0%

commit v1 on v0

v1 whole, which is shorter than its diff:
```python
import functools

import jax
import jax.numpy as jnp
from jax import lax
from jax.experimental import pallas as pl
from jax.experimental.pallas import tpu as pltpu
from jax.sharding import PartitionSpec as P

root_half = 0.7071067811865476
normal_density = 0.3989422804014327
momentum_decay = 0.9
second_decay = 0.95
stable_eps = 1e-08
weight_decay = 0.1
LANES = 128


def contract(left, right, left_dim, right_dim):
    return lax.dot_general(
        left, right, (((left_dim,), (right_dim,)), ((), ())), preferred_element_type=jnp.float32
    )


def activate(preact, hidden_grad):
    cumulative = 0.5 * (1.0 + lax.erf(preact * root_half))
    density = jnp.exp(-0.5 * preact * preact) * normal_density
    hidden = (preact * cumulative).astype(jnp.bfloat16)
    delta = (hidden_grad * (cumulative + preact * density)).astype(jnp.bfloat16)
    return (hidden, delta)


def exchange_kernel(plan, sizes, *refs):
    count = len(plan)
    sources, targets = refs[:count], refs[count : 2 * count]
    send_sem, recv_sem, own_sem = refs[2 * count :]
    axes = sorted(set(axis for axis, _ in plan))
    me = {axis: lax.axis_index(axis) for axis in axes}
    barrier = pltpu.get_barrier_semaphore()
    greeted = 0
    for axis in axes:
        for step in range(1, sizes[axis]):
            peer = lax.rem(me[axis] + step, sizes[axis])
            pl.semaphore_signal(
                barrier, inc=1, device_id={axis: peer}, device_id_type=pl.DeviceIdType.MESH
            )
            greeted += 1
    owns = []
    for item, (axis, scatter) in enumerate(plan):
        block = sources[item].at[me[axis]] if scatter else sources[item]
        own = pltpu.make_async_copy(block, targets[item].at[me[axis]], own_sem.at[item])
        own.start()
        owns.append(own)
    pl.semaphore_wait(barrier, greeted)
    copies = []
    at = 0
    for item, (axis, scatter) in enumerate(plan):
        for step in range(1, sizes[axis]):
            peer = lax.rem(me[axis] + step, sizes[axis])
            block = sources[item].at[peer] if scatter else sources[item]
            copy = pltpu.make_async_remote_copy(
                src_ref=block,
                dst_ref=targets[item].at[me[axis]],
                send_sem=send_sem.at[at],
                recv_sem=recv_sem.at[at],
                device_id={axis: peer},
                device_id_type=pl.DeviceIdType.MESH,
            )
            copy.start()
            copies.append(copy)
            at += 1
    for own in owns:
        own.wait()
    for copy in copies:
        copy.wait()


def exchange(identity, plan, sizes, *arrays):
    flights = sum(sizes[axis] - 1 for axis, _ in plan)
    shapes = [
        jax.ShapeDtypeStruct(
            array.shape if scatter else (sizes[axis],) + array.shape, array.dtype
        )
        for array, (axis, scatter) in zip(arrays, plan)
    ]
    return pl.pallas_call(
        functools.partial(exchange_kernel, plan, sizes),
        out_shape=shapes,
        in_specs=[pl.BlockSpec(memory_space=pl.ANY)] * len(plan),
        out_specs=[pl.BlockSpec(memory_space=pl.ANY)] * len(plan),
        scratch_shapes=[
            pltpu.SemaphoreType.DMA((flights,)),
            pltpu.SemaphoreType.DMA((flights,)),
            pltpu.SemaphoreType.DMA((len(plan),)),
        ],
        compiler_params=pltpu.CompilerParams(collective_id=identity, has_side_effects=True),
        name=f"exchange{identity}",
    )(*arrays)


def lane_fold(values, combine):
    folded = values[:, :LANES]
    for at in range(LANES, values.shape[1], LANES):
        folded = combine(folded, values[:, at : at + LANES])
    return folded


def squares_kernel(left_ref, right_ref, total_ref):
    gradient = contract(left_ref[...], right_ref[...], 0, 0)
    folded = lane_fold(gradient * gradient, jnp.add)
    folded = jnp.sum(folded.reshape(-1, 8, LANES), axis=0)

    @pl.when(pl.program_id(0) == 0)
    def _():
        total_ref[...] = jnp.zeros_like(total_ref)

    total_ref[...] += folded


def row_block(rows):
    return 256 if rows % 256 == 0 else 128


def squares(left, right):
    tokens, rows = left.shape
    block = row_block(rows)
    return pl.pallas_call(
        squares_kernel,
        grid=(rows // block,),
        out_shape=jax.ShapeDtypeStruct((8, LANES), jnp.float32),
        in_specs=[
            pl.BlockSpec((tokens, block), lambda i: (0, i)),
            pl.BlockSpec(right.shape, lambda i: (0, 0)),
        ],
        out_specs=pl.BlockSpec((8, LANES), lambda i: (0, 0)),
        name="squares",
    )(left, right)


def to_lanes(column_tops):
    pieces = []
    for at in range(0, column_tops.shape[0], LANES):
        turned = column_tops[at : at + LANES].T
        pieces.append(jnp.max(turned, axis=0, keepdims=True))
    return jnp.concatenate(pieces, axis=1)


def moments_kernel(
    factor_ref, left_ref, right_ref, weight_ref, moment_ref, second_ref,
    update_ref, new_moment_ref, new_second_ref, row_ref, col_ref,
):
    gradient = contract(left_ref[...], right_ref[...], 0, 0)
    scaled = gradient * factor_ref[0, 0]
    moment_new = momentum_decay * moment_ref[...].astype(jnp.float32) + (
        1.0 - momentum_decay
    ) * scaled
    second_new = second_decay * second_ref[...].astype(jnp.float32) + (
        1.0 - second_decay
    ) * scaled * scaled
    update = moment_new / (jnp.sqrt(second_new) + stable_eps) + weight_decay * weight_ref[
        ...
    ].astype(jnp.float32)
    update_ref[...] = update.astype(jnp.bfloat16)
    new_moment_ref[...] = moment_new.astype(jnp.bfloat16)
    new_second_ref[...] = second_new.astype(jnp.bfloat16)
    size = jnp.abs(moment_new)
    row_ref[0:1, :] = to_lanes(lane_fold(size, jnp.maximum))
    row_ref[1:2, :] = to_lanes(lane_fold(second_new, jnp.maximum))

    @pl.when(pl.program_id(0) == 0)
    def _():
        col_ref[...] = jnp.zeros_like(col_ref)

    col_ref[0:1, :] = jnp.maximum(col_ref[0:1, :], jnp.max(size, axis=0, keepdims=True))
    col_ref[1:2, :] = jnp.maximum(col_ref[1:2, :], jnp.max(second_new, axis=0, keepdims=True))


def moments(factor, left, right, weight, moment, second):
    rows, cols = weight.shape
    tokens = left.shape[0]
    block = row_block(rows)
    tile = pl.BlockSpec((block, cols), lambda i: (i, 0))
    half = jax.ShapeDtypeStruct((rows, cols), jnp.bfloat16)
    return pl.pallas_call(
        moments_kernel,
        grid=(rows // block,),
        out_shape=[
            half,
            half,
            half,
            jax.ShapeDtypeStruct((2, rows), jnp.float32),
            jax.ShapeDtypeStruct((2, cols), jnp.float32),
        ],
        in_specs=[
            pl.BlockSpec(memory_space=pltpu.SMEM),
            pl.BlockSpec((tokens, block), lambda i: (0, i)),
            pl.BlockSpec((tokens, cols), lambda i: (0, 0)),
            tile,
            tile,
            tile,
        ],
        out_specs=[
            tile,
            tile,
            tile,
            pl.BlockSpec((2, block), lambda i: (0, i)),
            pl.BlockSpec((2, cols), lambda i: (0, 0)),
        ],
        name="moments",
    )(factor, left, right, weight, moment, second)


def encode_kernel(moment_ref, second_ref, row_ref, col_ref, code_moment_ref, code_second_ref):
    rows, cols = moment_ref.shape
    for which, (source, target) in enumerate(
        ((moment_ref, code_moment_ref), (second_ref, code_second_ref))
    ):
        for low in range(0, rows, LANES):
            span = pl.ds(low, LANES)
            inverse = 1.0 / row_ref[which : which + 1, low : low + LANES]
            inverse = jnp.broadcast_to(inverse, (LANES, LANES)).T
            for at in range(0, cols, LANES):
                other = 1.0 / col_ref[which : which + 1, at : at + LANES]
                value = source[span, at : at + LANES].astype(jnp.float32)
                target[span, at : at + LANES] = (value * jnp.maximum(inverse, other)).astype(
                    jnp.bfloat16
                )


def encode(moment, second, row_top, col_top):
    rows, cols = moment.shape
    block = row_block(rows)
    tile = pl.BlockSpec((block, cols), lambda i: (i, 0))
    half = jax.ShapeDtypeStruct((rows, cols), jnp.bfloat16)
    return pl.pallas_call(
        encode_kernel,
        grid=(rows // block,),
        out_shape=[half, half],
        in_specs=[
            tile,
            tile,
            pl.BlockSpec((2, block), lambda i: (0, i)),
            pl.BlockSpec((2, cols), lambda i: (0, 0)),
        ],
        out_specs=[tile, tile],
        name="encode",
    )(moment, second, row_top, col_top)


def shards(
    sizes, inputs, cotangent, weight_in, moment_in, second_in, weight_out, moment_out, second_out
):
    rows, cols = sizes["row"], sizes["col"]
    width_in, hidden_cols = weight_in.shape
    width = inputs.shape[1]
    tokens = inputs.shape[0] * cols
    entries = 2.0 * width_in * rows * hidden_cols * cols
    all_inputs, all_cotangent = exchange(
        0, (("col", False), ("col", False)), sizes, inputs, cotangent
    )
    all_inputs = all_inputs.reshape(tokens, width)
    all_cotangent = all_cotangent.reshape(tokens, width)
    preact_part = contract(all_inputs, weight_in, 1, 0).astype(jnp.bfloat16)
    grad_part = contract(all_cotangent, weight_out, 1, 1).astype(jnp.bfloat16)
    parts = (rows, tokens // rows, hidden_cols)
    preact_parts, grad_parts = exchange(
        1,
        (("row", True), ("row", True)),
        sizes,
        preact_part.reshape(parts),
        grad_part.reshape(parts),
    )
    preact = jnp.sum(preact_parts.astype(jnp.float32), axis=0)
    hidden_grad = jnp.sum(grad_parts.astype(jnp.float32), axis=0)
    hidden, delta = activate(preact, hidden_grad)
    all_hidden, all_delta = exchange(2, (("row", False), ("row", False)), sizes, hidden, delta)
    all_hidden = all_hidden.reshape(tokens, hidden_cols)
    all_delta = all_delta.reshape(tokens, hidden_cols)
    grad_input_part = contract(all_delta, weight_in, 1, 1).astype(jnp.bfloat16)
    local_total = squares(all_inputs, all_delta) + squares(all_hidden, all_cotangent)
    grad_input_parts, totals = exchange(
        3,
        (("col", True), ("col", False)),
        sizes,
        grad_input_part.reshape(cols, tokens // cols, width),
        local_total,
    )
    input_grad = jnp.sum(grad_input_parts.astype(jnp.float32), axis=0).astype(jnp.bfloat16)
    (totals,) = exchange(4, (("row", False),), sizes, jnp.sum(totals, axis=0))
    total = jnp.sum(totals)
    factor = 1.0 / jnp.maximum(jnp.sqrt(total / entries), 1.0)
    factor = factor.reshape(1, 1)
    update_in, moment_new_in, second_new_in, rows_in, cols_in = moments(
        factor, all_inputs, all_delta, weight_in, moment_in, second_in
    )
    update_out, moment_new_out, second_new_out, rows_out, cols_out = moments(
        factor, all_hidden, all_cotangent, weight_out, moment_out, second_out
    )
    rows_in, cols_out, cols_in, rows_out = exchange(
        5,
        (("col", False), ("col", False), ("row", False), ("row", False)),
        sizes,
        rows_in,
        cols_out,
        cols_in,
        rows_out,
    )
    rows_in, cols_out, cols_in, rows_out = (
        jnp.maximum(jnp.max(tops, axis=0), 1.0) for tops in (rows_in, cols_out, cols_in, rows_out)
    )
    code_moment_in, code_second_in = encode(moment_new_in, second_new_in, rows_in, cols_in)
    code_moment_out, code_second_out = encode(moment_new_out, second_new_out, rows_out, cols_out)
    return (
        input_grad,
        update_in,
        code_moment_in,
        code_second_in,
        rows_in,
        cols_in,
        update_out,
        code_moment_out,
        code_second_out,
        rows_out,
        cols_out,
    )


def solution(mesh):
    in_specs = (
        P("col", "row"),
        P("col", "row"),
        P("row", "col"),
        P("row", "col"),
        P("row", "col"),
        P("col", "row"),
        P("col", "row"),
        P("col", "row"),
    )
    out_specs = (
        P("col", "row"),
        P("row", "col"),
        P("row", "col"),
        P("row", "col"),
        P(None, "row"),
        P(None, "col"),
        P("col", "row"),
        P("col", "row"),
        P("col", "row"),
        P(None, "col"),
        P(None, "row"),
    )
    sizes = {axis: mesh.shape[axis] for axis in ("row", "col")}
    return jax.shard_map(
        functools.partial(shards, sizes),
        mesh=mesh,
        in_specs=in_specs,
        out_specs=out_specs,
        check_vma=False,
    )
```

time: 434 us -> 299 us (0.69)
  Pallas kernels: 0 us -> 266 us
  waiting for transfers between devices: 147 us -> 0 us
  local copies, waits for them, and re-layouts: 89.8 us -> 0.03 us
  blocking collectives: 88.6 us -> 0 us
  other arithmetic: 57.8 us -> 14.4 us
  matrix products: 31.8 us -> 16.5 us
  between operations: 16.4 us -> 1.5 us
    pallas_call x0 -> x12, Pallas kernels: none -> 266 us  [the longest x6 201 us: exchange(): pl.pallas_call(functools.partial(exchange_kernel, plan, sizes), out_shape...]
    all_gather x4 -> x0, waiting for transfers between devices: 88.2 us -> none  [the longest x1 48.4 us: shards(): lax.all_gather(cotangent, 'col', axis=0, tiled=True)]
    unnamed x26 -> x14, local copies, waits for them, and re-layouts: 79.9 us -> 0.03 us
    reduce_scatter x2 -> x0, waiting for transfers between devices: 57.3 us -> none  [the longest x1 57.3 us: shards(): lax.psum_scatter(jnp.concatenate([preact_part, grad_part], axis=1), 'row'...]
    pmax x2 -> x0, blocking collectives: 46.9 us -> none  [the longest x1 36.4 us: shards(): rows_in, cols_out = lax.pmax((rows_in, cols_out), 'col')]
    psum x1 -> x0, blocking collectives: 41.7 us -> none  [shards(): total = lax.psum(local_total, ('row', 'col'))]
    reduce_max x2 -> x4, other arithmetic: 29.1 us -> 1.83 us  [shards(): jnp.max(tops, axis=0)]
    convert_element_type x3 -> x1, other arithmetic: 25.4 us -> 1.23 us  [activate(): delta = (hidden_grad * (cumulative + preact * density)).astype(jnp.bfloat16)]
  transfers between devices with their start and end apart: 6 -> 0, of which waited for: 3 -> 0; matrix products, arithmetic and copies ran while one was open for 35% -> 0% of each run, Pallas kernels for 0% -> 0%
where the time goes in v1:
time: 299 us; the launch traced here: 298 us
  Pallas kernels  266 us (89%)
  matrix products  16.5 us (6%)
  other arithmetic  14.4 us (5%)
    pallas_call x6, Pallas kernels, exchange(): pl.pallas_call(functools.partial(exchange_kernel, plan, sizes), out_shape...  201 us
    pallas_call x2, Pallas kernels, moments(): pl.pallas_call(moments_kernel, grid=(rows // block,), out_shape=[half, ha...  33.4 us
    pallas_call x2, Pallas kernels, encode(): pl.pallas_call(encode_kernel, grid=(rows // block,), out_shape=[half, hal...  18.5 us
    dot_general x3, matrix products, contract(): lax.dot_general(left, right, (((left_dim,), (right_dim,)), ((), ())), pre...  16.5 us
    pallas_call x2, Pallas kernels, squares(): pl.pallas_call(squares_kernel, grid=(rows // block,), out_shape=jax.Shape...  13.1 us

profile of v1, /device:TPU:0, one launch (start us, length us, event | category | flops | bytes accessed | tf_op | source)
XLA Modules:
  0.0 298.3 jit_solution(17208676402667381505)
XLA Ops:
  0.7 62.7 %exchange0.1 = (bf16[8,64,1536]{2,1,0:T(8,128)(2,1)}, bf16[8,64,1536]{2,1,0:T(8,128)(2,1)}) custom-call(bf16[64,1536]{1,0:T(8,128)(2,1)} %refs_0_.1, bf16[64,1536]{1,0:T(8,128)(2,1)} %refs_1_.1), custom_call_target="tpu_custom_call" | custom-call | tf_op jit(solution)/shard_map/exchange0/pallas_call | solution.py:86
  63.4 6.7 %convolution_convert_fusion.1 = bf16[512,1536]{1,0:T(8,128)(2,1)} fusion(bf16[512,1536]{1,0:T(8,128)(2,1)} %bitcast.17, bf16[1536,1536]{1,0:T(8,128)(2,1)} %weight_ref.3), kind=kOutput, calls=%fused_computation.3 | convolution fusion | flops 2416705536 | bytes 7864320 | tf_op jit(solution)/shard_map/dot_general | solution.py:20
  70.2 3.7 %convolution_convert_fusion.2 = bf16[512,1536]{1,0:T(8,128)(2,1)} fusion(bf16[512,1536]{1,0:T(8,128)(2,1)S(1)} %bitcast.16, bf16[1536,1536]{1,0:T(8,128)(2,1)S(1)} %bitcast.26), kind=kOutput, calls=%fused_computation.4 | convolution fusion | flops 2416705536 | bytes 7864320 | tf_op jit(solution)/shard_map/dot_general | solution.py:20
  73.9 36.1 %exchange1.1 = (bf16[4,128,1536]{2,1,0:T(8,128)(2,1)}, bf16[4,128,1536]{2,1,0:T(8,128)(2,1)}) custom-call(bf16[4,128,1536]{2,1,0:T(8,128)(2,1)} %bitcast.28, bf16[4,128,1536]{2,1,0:T(8,128)(2,1)} %bitcast.27), custom_call_target="tpu_custom_call" | custom-call | tf_op jit(solution)/shard_map/exchange1/pallas_call | solution.py:86
  110.0 2.6 convert_reduce_fusion
  112.6 1.2 fusion.5
  113.8 36.6 %exchange2.1 = (bf16[4,128,1536]{2,1,0:T(8,128)(2,1)}, bf16[4,128,1536]{2,1,0:T(8,128)(2,1)}) custom-call(bf16[128,1536]{1,0:T(8,128)(2,1)} %get-tuple-element.64.refs_0_, bf16[128,1536]{1,0:T(8,128)(2,1)} %get-tuple-element.63.refs_1_), custom_call_target="tpu_custom_call" | custom-call | tf_op jit(solution)/shard_map/exchange2/pallas_call | solution.py:86
  150.4 6.6 %squares.3 = f32[8,128]{1,0:T(8,128)} custom-call(bf16[512,1536]{1,0:T(8,128)(2,1)} %bitcast.23, bf16[512,1536]{1,0:T(8,128)(2,1)} %bitcast.18), custom_call_target="tpu_custom_call" | custom-call | tf_op jit(solution)/shard_map/squares/pallas_call | solution.py:127
  157.0 6.5 %squares.2 = f32[8,128]{1,0:T(8,128)} custom-call(bf16[512,1536]{1,0:T(8,128)(2,1)} %bitcast.14, bf16[512,1536]{1,0:T(8,128)(2,1)} %bitcast.20), custom_call_target="tpu_custom_call" | custom-call | tf_op jit(solution)/shard_map/squares/pallas_call | solution.py:127
  163.5 1.3 add.15.refs_1_
  164.8 6.1 %convolution_convert_fusion = bf16[512,1536]{1,0:T(8,128)(2,1)} fusion(bf16[512,1536]{1,0:T(8,128)(2,1)S(1)} %bitcast.22, bf16[1536,1536]{1,0:T(8,128)(2,1)} %weight_ref.2), kind=kOutput, calls=%fused_computation.2 | convolution fusion | flops 2416705536 | bytes 7864320 | tf_op jit(solution)/shard_map/dot_general | solution.py:20
  170.8 52.6 %exchange3.1 = (bf16[8,64,1536]{2,1,0:T(8,128)(2,1)}, f32[8,8,128]{2,1,0:T(8,128)}) custom-call(bf16[8,64,1536]{2,1,0:T(8,128)(2,1)} %bitcast.29, f32[8,128]{1,0:T(8,128)} %add.15.refs_1_), custom_call_target="tpu_custom_call" | custom-call | tf_op jit(solution)/shard_map/exchange3/pallas_call | solution.py:86
  223.5 2.4 reduce_sum.50
  225.8 1.4 reduce_sum.51.refs_0_
  227.2 4.0 %exchange4.1 = f32[4,8,128]{2,1,0:T(8,128)} custom-call(f32[8,128]{1,0:T(8,128)} %reduce_sum.51.refs_0_), custom_call_target="tpu_custom_call" | custom-call | tf_op jit(solution)/shard_map/exchange4/pallas_call | solution.py:86
  231.2 1.3 reduce_sum.52
  233.3 16.8 %moments.3 = (bf16[1536,1536]{1,0:T(8,128)(2,1)}, bf16[1536,1536]{1,0:T(8,128)(2,1)}, bf16[1536,1536]{1,0:T(8,128)(2,1)}, f32[2,1536]{1,0:T(2,128)}, f32[2,1536]{1,0:T(2,128)}) custom-call(f32[1,1]{1,0:T(1,128)} %bitcast.7.factor_ref, bf16[512,1536]{1,0:T(8,128)(2,1)} %bitcast.24, bf16[512,1536]{1,0:T(8,128)(2,1)} %bitcast.19, ...), custom_call_target="tpu_custom_call" | custom-call | tf_op jit(solution)/shard_map/moments/pallas_call | solution.py:184
  250.0 16.7 %moments.2 = (bf16[1536,1536]{1,0:T(8,128)(2,1)}, bf16[1536,1536]{1,0:T(8,128)(2,1)}, bf16[1536,1536]{1,0:T(8,128)(2,1)}, f32[2,1536]{1,0:T(2,128)}, f32[2,1536]{1,0:T(2,128)}) custom-call(f32[1,1]{1,0:T(1,128)} %bitcast.7.factor_ref, bf16[512,1536]{1,0:T(8,128)(2,1)} %bitcast.15, bf16[512,1536]{1,0:T(8,128)(2,1)} %bitcast.21, ...), custom_call_target="tpu_custom_call" | custom-call | tf_op jit(solution)/shard_map/moments/pallas_call | solution.py:184
  266.7 8.8 %exchange5.1 = (f32[8,2,1536]{2,1,0:T(2,128)}, f32[8,2,1536]{2,1,0:T(2,128)}, f32[4,2,1536]{2,1,0:T(2,128)}, f32[4,2,1536]{2,1,0:T(2,128)}) custom-call(f32[2,1536]{1,0:T(2,128)} %get-tuple-element.48.refs_0_, f32[2,1536]{1,0:T(2,128)} %get-tuple-element.49.refs_1_, f32[2,1536]{1,0:T(2,128)} %get-tuple-element.50.refs_2_, f32[2,1536]{1,0:T(2,128)} %get-tuple-element.51.refs_3_), custom_call_target="tpu_custom_call" | custom-call | tf_op jit(solution)/shard_map/exchange5/pallas_call | solution.py:86
  275.5 0.9 reduce_max.36
  277.1 0.8 reduce_max.37
  278.5 9.3 %encode.2 = (bf16[1536,1536]{1,0:T(8,128)(2,1)}, bf16[1536,1536]{1,0:T(8,128)(2,1)}) custom-call(bf16[1536,1536]{1,0:T(8,128)(2,1)} %get-tuple-element.46.moment_ref, bf16[1536,1536]{1,0:T(8,128)(2,1)} %get-tuple-element.47.second_ref, f32[2,1536]{1,0:T(2,128)} %broadcast_maximum_fusion.3.row_ref, f32[2,1536]{1,0:T(2,128)} %broadcast_maximum_fusion.2.col_ref), custom_call_target="tpu_custom_call" | custom-call | tf_op jit(solution)/shard_map/encode/pallas_call | solution.py:235
  287.9 0.6 broadcast_maximum_fusion.col_ref
  289.1 9.2 %encode.3 = (bf16[1536,1536]{1,0:T(8,128)(2,1)}, bf16[1536,1536]{1,0:T(8,128)(2,1)}) custom-call(bf16[1536,1536]{1,0:T(8,128)(2,1)} %get-tuple-element.57.moment_ref, bf16[1536,1536]{1,0:T(8,128)(2,1)} %get-tuple-element.58.second_ref, f32[2,1536]{1,0:T(2,128)} %broadcast_maximum_fusion.1.row_ref, f32[2,1536]{1,0:T(2,128)} %broadcast_maximum_fusion.col_ref), custom_call_target="tpu_custom_call" | custom-call | tf_op jit(solution)/shard_map/encode/pallas_call | solution.py:235
  (20 shorter events, 1.9 us)
Async XLA Ops:
  0.6 69.5 %slice-start = ((s8[4718592]{0:T(1024)(128)(4,1)}), s8[524288]{0:T(1024)(128)(4,1)S(1)}, s32[]{:S(2)}) async-start(s8[4718592]{0:T(1024)(128)(4,1)} %bitcast.25), calls=%async_computation | async-start | bytes 1048576
  63.4 6.8 %copy-start = (bf16[8,64,1536]{2,1,0:T(8,128)(2,1)S(1)}, bf16[8,64,1536]{2,1,0:T(8,128)(2,1)}, u32[]{:S(2)}) copy-start(bf16[8,64,1536]{2,1,0:T(8,128)(2,1)} %get-tuple-element.37) | copy-start | bytes 4718596
  63.4 6.8 %slice-start.1 = ((s8[4718592]{0:T(1024)(128)(4,1)}), s8[4194304]{0:T(1024)(128)(4,1)S(1)}, s32[]{:S(2)}) async-start(s8[4718592]{0:T(1024)(128)(4,1)} %bitcast.25), calls=%async_computation.1 | async-start | bytes 8388608
  150.4 14.4 %copy-start.1 = (bf16[4,128,1536]{2,1,0:T(8,128)(2,1)S(1)}, bf16[4,128,1536]{2,1,0:T(8,128)(2,1)}, u32[]{:S(2)}) copy-start(bf16[4,128,1536]{2,1,0:T(8,128)(2,1)} %get-tuple-element.41) | copy-start | bytes 4718596
  157.0 6.5 %copy-start.4 = (f32[8,128]{1,0:T(8,128)S(1)}, f32[8,128]{1,0:T(8,128)}, u32[]{:S(2)}) copy-start(f32[8,128]{1,0:T(8,128)} %squares.3) | copy-start | bytes 12292
  278.5 9.3 %copy-start.3 = (f32[4,2,1536]{2,1,0:T(2,128)S(1)}, f32[4,2,1536]{2,1,0:T(2,128)}, u32[]{:S(2)}) copy-start(f32[4,2,1536]{2,1,0:T(2,128)} %get-tuple-element.59) | copy-start | bytes 147460
  278.5 9.3 %copy-start.2 = (f32[8,2,1536]{2,1,0:T(2,128)S(1)}, f32[8,2,1536]{2,1,0:T(2,128)}, u32[]{:S(2)}) copy-start(f32[8,2,1536]{2,1,0:T(2,128)} %get-tuple-element.60) | copy-start | bytes 294916
